TPU v7x, 256 devices: a whole 4x4x8 slice. The times are simulated.
256 devices in a mesh: dp: 8 (over x, z_hi), pipe: 4 (over z_lo), expert: 8 (over y, core).
Axes of the slice: x: 4, y: 4, z: 8 (z_hi: 2, z_lo: 4; z = z_hi * 4 + z_lo), core: 2. Of those that a mesh axis runs over, the one named last changes fastest.
Arguments:
- tokens: bfloat16 [8192, 2048], P(('dp', 'expert')), may hold values from -6 to 6
- cotangent: bfloat16 [8192, 2048], P(('dp', 'expert')), may hold values from -6 to 6
- owner_ids: int32 [4, 8192, 4], P('pipe', ('dp', 'expert')), may hold values from 0 to 63, all different within a row; in each aligned block of 32 rows (0 to 31, 32 to 63, ..., all dimensions but the last counted through in order) at most 3 rows name the same one
- gate_weights: bfloat16 [4, 8192, 4], P('pipe', ('dp', 'expert')), may hold values from 0.049804688 to 0.25
- norm_gain: float32 [4, 2048], P('pipe'), may hold values from 0.5 to 1.5
- w_gate: bfloat16 [4, 64, 2048, 384], P('pipe', ('dp', 'expert')), may hold values from -0.125 to 0.125
- w_up: bfloat16 [4, 64, 2048, 384], P('pipe', ('dp', 'expert')), may hold values from -0.125 to 0.125
- w_down: bfloat16 [4, 64, 384, 2048], P('pipe', ('dp', 'expert')), may hold values from -0.3125 to 0.3125
Outputs:
- segment_out: bfloat16 [4, 8192, 2048], P('pipe', ('dp', 'expert'))
- segment_grad: bfloat16 [4, 8192, 2048], P('pipe', ('dp', 'expert'))
- gain_grad: float32 [4, 2048], P('pipe')
Inputs may be any that keep to these rules, and one draw needn't show every extreme that they name: `owner_ids`: each row names 4 different owners. In each aligned block of 32 rows (layers in order, then tokens) no owner is named by more than 3 rows, and that bound is reached.
All inputs are finite; a program needn't handle non-finite values.
Results may differ from a plain program's by a relative error of at most 0.014.
Values may be sent and summed in bfloat16 or wider, within the bound.
A program may use at most 128 MiB of HBM per device.

v0:
```python
import jax
import jax.numpy as jnp
from jax import lax
from jax.sharding import PartitionSpec as P

MICRO = 4
epsilon = 1e-06


def from_behind(value, axis, steps):
    count = lax.axis_size(axis)
    leading, last = (max(0, -steps), min(count, count - steps))
    return lax.ppermute(value, axis, [(source, source + steps) for source in range(leading, last)])


def inverse_rms(values):
    return lax.rsqrt(jnp.mean(values * values, axis=-1, keepdims=True) + epsilon)


def contract_last(left, right):
    return lax.dot_general(
        left, right, (((1,), (1,)), ((), ())), preferred_element_type=jnp.float32
    )


def route_tables(ids_part, owners, capacity):
    owner_range = jnp.arange(owners, dtype=jnp.int32)
    onehot = (ids_part[:, :, None] == owner_range[None, None, :]).astype(jnp.int32)
    member = jnp.sum(onehot, axis=1)
    position = jnp.cumsum(member, axis=0) - member
    slot_range = jnp.arange(capacity, dtype=jnp.int32)
    placed = (position[:, :, None] == slot_range[None, None, :]) & (member[:, :, None] > 0)
    placing = jnp.transpose(placed, (1, 2, 0)).astype(jnp.bfloat16)
    return (onehot.astype(jnp.float32), placing)


def gate_slots(onehot, gates_part, placing, experts_here):
    gate_pairs = gates_part.astype(jnp.float32).reshape(gates_part.shape[0], -1, experts_here)
    chosen = jnp.einsum("rjo,rjc->roc", onehot, gate_pairs)
    return jnp.einsum("okr,roc->okc", placing.astype(jnp.float32), chosen).astype(jnp.bfloat16)


def send_rows(row_block, pair_block):
    got_rows, got_pairs = (
        lax.all_to_all(row_block, ("dp", "expert"), split_axis=0, concat_axis=0, tiled=True),
        lax.all_to_all(pair_block, ("dp", "expert"), split_axis=0, concat_axis=0, tiled=True),
    )
    return (got_rows, got_pairs)


def return_rows(row_block):
    return lax.all_to_all(row_block, ("dp", "expert"), split_axis=0, concat_axis=0, tiled=True)


def send_grads(row_block):
    return lax.all_to_all(row_block, ("dp", "expert"), split_axis=0, concat_axis=0, tiled=True)


def return_grads(row_block):
    return lax.all_to_all(row_block, ("dp", "expert"), split_axis=0, concat_axis=0, tiled=True)


def expert_forward(flat_rows, flat_pairs, joint_mats, down_mats):
    hidden_width = down_mats.shape[1]
    joint_pre = jnp.dot(flat_rows, joint_mats[0], preferred_element_type=jnp.float32)
    gate_pre = joint_pre[:, :hidden_width]
    up_pre = joint_pre[:, hidden_width:]
    hidden = (jax.nn.silu(gate_pre) * up_pre).astype(jnp.bfloat16)
    projected = jnp.dot(hidden, down_mats[0], preferred_element_type=jnp.float32)
    term = flat_pairs.astype(jnp.float32) * projected
    kept_both = [joint_pre]
    return (term.astype(jnp.bfloat16), jnp.stack(kept_both))


def expert_backward(grad_rows, flat_pairs, joint_keep, joint_mats, down_mats):
    hidden_width = down_mats.shape[1]
    q_vals = contract_last(grad_rows, down_mats[0])
    gate_pre = joint_keep[0][:, :hidden_width]
    up_pre = joint_keep[0][:, hidden_width:]
    sigma = jax.nn.sigmoid(gate_pre)
    weight = flat_pairs.astype(jnp.float32)
    d_gate = (q_vals * weight * up_pre * sigma * (1.0 + gate_pre * (1.0 - sigma))).astype(
        jnp.bfloat16
    )
    d_up = (q_vals * weight * gate_pre * sigma).astype(jnp.bfloat16)
    joint_grad = jnp.concatenate([d_gate, d_up], axis=1)
    term = contract_last(joint_grad, joint_mats[0])
    return term.astype(jnp.bfloat16)


def body(tokens, cotangent, owner_ids, gate_weights, norm_gain, w_gate, w_up, w_down):
    segments = lax.axis_size("pipe")
    segment_index = lax.axis_index("pipe")
    owners = lax.axis_size("dp") * lax.axis_size("expert")
    tok_rows = tokens.shape[0]
    width = tokens.shape[1]
    micro_rows = tok_rows // MICRO
    route_count = owner_ids.shape[2]
    capacity = max(2, (5 * micro_rows * route_count + 4 * owners - 1) // (4 * owners))
    slot_count = owners * capacity
    gain_row = norm_gain[0]
    joint_mats = jnp.concatenate([w_gate[0], w_up[0]], axis=2)
    down_mats = w_down[0]
    layer_ids = owner_ids[0]
    layer_gates = gate_weights[0]
    experts_here = joint_mats.shape[0]
    joint_width = joint_mats.shape[2]

    def skip_forward(operands):
        return (
            jnp.zeros((slot_count, width), jnp.bfloat16),
            jnp.zeros((experts_here, slot_count, joint_width), jnp.float32),
        )

    def run_forward(operands):
        return expert_forward(operands[0], operands[1], joint_mats, down_mats)

    def skip_backward(operands):
        return jnp.zeros((slot_count, width), jnp.bfloat16)

    def run_backward(operands):
        return expert_backward(operands[0], operands[1], operands[2], joint_mats, down_mats)

    def timing(micro):
        is_valid = (micro >= 0) & (micro < MICRO)
        slot_pick = jnp.where(is_valid, micro, MICRO)
        start_row = jnp.clip(micro, 0, MICRO - 1) * micro_rows
        return (is_valid, slot_pick, start_row)

    layer_outs = jnp.zeros((MICRO + 1, micro_rows, width), jnp.bfloat16)
    layer_ins = jnp.zeros((MICRO + 1, micro_rows, width), jnp.bfloat16)
    kept_joint = jnp.zeros((MICRO + 1, experts_here, slot_count, joint_width), jnp.float32)
    kept_pairs = jnp.zeros((MICRO + 1, slot_count, experts_here), jnp.bfloat16)
    grad_outs = jnp.zeros((MICRO + 1, micro_rows, width), jnp.bfloat16)
    gain_sum = jnp.zeros((width,), jnp.float32)
    ticks = MICRO + segments - 1
    incoming = jnp.zeros((micro_rows, width), jnp.bfloat16)
    for tick_num in range(ticks):
        forward_is_valid, forward_slot_pick, forward_start_row = timing(tick_num - segment_index)
        forward_own_part = lax.dynamic_slice_in_dim(tokens, forward_start_row, micro_rows, 0)
        forward_layer_in = jnp.where(segment_index == 0, forward_own_part, incoming)
        forward_ids_part = lax.dynamic_slice_in_dim(layer_ids, forward_start_row, micro_rows, 0)
        gates_part = lax.dynamic_slice_in_dim(layer_gates, forward_start_row, micro_rows, 0)
        forward_x_float = forward_layer_in.astype(jnp.float32)
        forward_scale = inverse_rms(forward_x_float)
        normed = (forward_x_float * forward_scale * gain_row).astype(jnp.bfloat16)
        forward_onehot, forward_placing = route_tables(forward_ids_part, owners, capacity)
        row_block = jnp.einsum(
            "okr,rd->okd", forward_placing, normed, preferred_element_type=jnp.float32
        ).astype(jnp.bfloat16)
        pair_block = gate_slots(forward_onehot, gates_part, forward_placing, experts_here)
        f_valid, f_pick, layer_in, x_float, f_placing, row_block, pair_block = (
            forward_is_valid,
            forward_slot_pick,
            forward_layer_in,
            forward_x_float,
            forward_placing,
            row_block,
            pair_block,
        )
        got_rows, got_pairs = send_rows(row_block, pair_block)
        flat_rows = got_rows.reshape(slot_count, width)
        flat_pairs = got_pairs.reshape(slot_count, experts_here)
        result, joint_pre = lax.cond(f_valid, run_forward, skip_forward, (flat_rows, flat_pairs))
        returned = return_rows(result.reshape(owners, capacity, width))
        branch = jnp.einsum("okr,okd->rd", f_placing, returned, preferred_element_type=jnp.float32)
        layer_out = (x_float + branch).astype(jnp.bfloat16)
        layer_outs = lax.dynamic_update_index_in_dim(layer_outs, layer_out, f_pick, 0)
        layer_ins = lax.dynamic_update_index_in_dim(layer_ins, layer_in, f_pick, 0)
        kept_joint = lax.dynamic_update_index_in_dim(kept_joint, joint_pre, f_pick, 0)
        kept_pairs = lax.dynamic_update_index_in_dim(kept_pairs, flat_pairs, f_pick, 0)
        if tick_num + 1 < ticks:
            incoming = from_behind(layer_out, "pipe", 1)
    incoming = jnp.zeros((micro_rows, width), jnp.bfloat16)
    for tick_num in range(ticks):
        backward_is_valid, backward_slot_pick, backward_start_row = timing(
            tick_num - (segments - 1 - segment_index)
        )
        own_part = lax.dynamic_slice_in_dim(cotangent, backward_start_row, micro_rows, 0)
        backward_grad_in = jnp.where(segment_index == segments - 1, own_part, incoming)
        ids_part = lax.dynamic_slice_in_dim(layer_ids, backward_start_row, micro_rows, 0)
        backward_layer_in = lax.dynamic_index_in_dim(
            layer_ins, backward_slot_pick, 0, keepdims=False
        )
        backward_x_float = backward_layer_in.astype(jnp.float32)
        backward_scale = inverse_rms(backward_x_float)
        onehot, backward_placing = route_tables(ids_part, owners, capacity)
        grad_block = jnp.einsum(
            "okr,rd->okd", backward_placing, backward_grad_in, preferred_element_type=jnp.float32
        ).astype(jnp.bfloat16)
        b_valid, b_pick, grad_in, bx_float, b_scale, b_placing, grad_block = (
            backward_is_valid,
            backward_slot_pick,
            backward_grad_in,
            backward_x_float,
            backward_scale,
            backward_placing,
            grad_block,
        )
        got_grads = send_grads(grad_block).reshape(slot_count, width)
        joint_keep = lax.dynamic_index_in_dim(kept_joint, b_pick, 0, keepdims=False)
        pair_keep = lax.dynamic_index_in_dim(kept_pairs, b_pick, 0, keepdims=False)
        owner_grad = lax.cond(
            b_valid, run_backward, skip_backward, (got_grads, pair_keep, joint_keep)
        )
        returned = return_grads(owner_grad.reshape(owners, capacity, width))
        normed_grad = jnp.einsum(
            "okr,okd->rd", b_placing, returned, preferred_element_type=jnp.float32
        )
        weighted = gain_row * normed_grad
        grad_x = (
            grad_in.astype(jnp.float32)
            + b_scale * weighted
            - bx_float
            * b_scale
            * b_scale
            * b_scale
            * jnp.mean(weighted * bx_float, axis=-1, keepdims=True)
        )
        gain_term = jnp.where(b_valid, jnp.sum(normed_grad * bx_float * b_scale, axis=0), 0.0)
        grad_bf, gain_term = (grad_x.astype(jnp.bfloat16), gain_term)
        grad_outs = lax.dynamic_update_index_in_dim(grad_outs, grad_bf, b_pick, 0)
        gain_sum = gain_sum + gain_term
        if tick_num + 1 < ticks:
            incoming = from_behind(grad_bf, "pipe", -1)
    gain_grad = lax.psum(gain_sum, ("dp", "expert"))
    segment_out = layer_outs[:MICRO].reshape(1, tok_rows, width)
    segment_grad = grad_outs[:MICRO].reshape(1, tok_rows, width)
    return (segment_out, segment_grad, gain_grad.reshape(1, width))


def solution(mesh):
    in_specs = (
        P(("dp", "expert"), None),
        P(("dp", "expert"), None),
        P("pipe", ("dp", "expert"), None),
        P("pipe", ("dp", "expert"), None),
        P("pipe", None),
        P("pipe", ("dp", "expert"), None, None),
        P("pipe", ("dp", "expert"), None, None),
        P("pipe", ("dp", "expert"), None, None),
    )
    out_specs = (
        P("pipe", ("dp", "expert"), None),
        P("pipe", ("dp", "expert"), None),
        P("pipe", None),
    )
    return jax.shard_map(body, mesh=mesh, in_specs=in_specs, out_specs=out_specs, check_vma=False)
```

profile of v0, /device:TPU:1, one launch (start us, length us, event | category | flops | bytes accessed | tf_op | source)
XLA Modules:
  0.0 1507.8 jit_solution(17595029229092546663)
XLA Ops:
  40.4 25.5 %all-to-all-done.1 = bf16[64,3,2048]{2,1,0:T(4,128)(2,1)} async-done(((bf16[64,3,2048]{2,1,0:T(4,128)(2,1)}), bf16[64,3,2048]{2,1,0:T(4,128)(2,1)}, u32[]{:S(2)}, u32[]{:S(2)}) %all-to-all-start.1) | async-done | bytes 786464 | tf_op jit(solution)/shard_map/all_to_all | solution.py:45
  136.9 28.5 %all-to-all-done.4 = bf16[64,3,2048]{2,1,0:T(4,128)(2,1)} async-done(((bf16[64,3,2048]{2,1,0:T(4,128)(2,1)}), bf16[64,3,2048]{2,1,0:T(4,128)(2,1)}, u32[]{:S(2)}, u32[]{:S(2)}) %all-to-all-start.4) | async-done | bytes 786464 | tf_op jit(solution)/shard_map/all_to_all | solution.py:45
  246.7 28.6 %all-to-all-done.7 = bf16[64,3,2048]{2,1,0:T(4,128)(2,1)} async-done(((bf16[64,3,2048]{2,1,0:T(4,128)(2,1)}), bf16[64,3,2048]{2,1,0:T(4,128)(2,1)}, u32[]{:S(2)}, u32[]{:S(2)}) %all-to-all-start.7) | async-done | bytes 786464 | tf_op jit(solution)/shard_map/all_to_all | solution.py:45
  298.6 20.2 %all-to-all-done.8 = bf16[64,3,2048]{2,1,0:T(4,128)(2,1)} async-done(((bf16[64,3,2048]{2,1,0:T(4,128)(2,1)}), bf16[64,3,2048]{2,1,0:T(4,128)(2,1)}, u32[]{:S(2)}, u32[]{:S(2)}) %all-to-all-start.8) | async-done | bytes 786464 | tf_op jit(solution)/shard_map/all_to_all | solution.py:52
  350.9 26.9 %all-to-all-done.10 = bf16[64,3,2048]{2,1,0:T(4,128)(2,1)} async-done(((bf16[64,3,2048]{2,1,0:T(4,128)(2,1)}), bf16[64,3,2048]{2,1,0:T(4,128)(2,1)}, u32[]{:S(2)}, u32[]{:S(2)}) %all-to-all-start.10) | async-done | bytes 786464 | tf_op jit(solution)/shard_map/all_to_all | solution.py:45
  399.7 21.5 %all-to-all-done.11 = bf16[64,3,2048]{2,1,0:T(4,128)(2,1)} async-done(((bf16[64,3,2048]{2,1,0:T(4,128)(2,1)}), bf16[64,3,2048]{2,1,0:T(4,128)(2,1)}, u32[]{:S(2)}, u32[]{:S(2)}) %all-to-all-start.11) | async-done | bytes 786464 | tf_op jit(solution)/shard_map/all_to_all | solution.py:52
  452.8 21.8 %all-to-all-done.13 = bf16[64,3,2048]{2,1,0:T(4,128)(2,1)} async-done(((bf16[64,3,2048]{2,1,0:T(4,128)(2,1)}), bf16[64,3,2048]{2,1,0:T(4,128)(2,1)}, u32[]{:S(2)}, u32[]{:S(2)}) %all-to-all-start.13) | async-done | bytes 786464 | tf_op jit(solution)/shard_map/all_to_all | solution.py:45
  486.5 24.1 %all-to-all-done.14 = bf16[64,3,2048]{2,1,0:T(4,128)(2,1)} async-done(((bf16[64,3,2048]{2,1,0:T(4,128)(2,1)}), bf16[64,3,2048]{2,1,0:T(4,128)(2,1)}, u32[]{:S(2)}, u32[]{:S(2)}) %all-to-all-start.14) | async-done | bytes 786464 | tf_op jit(solution)/shard_map/all_to_all | solution.py:52
  542.1 22.4 %all-to-all-done.16 = bf16[64,3,2048]{2,1,0:T(4,128)(2,1)} async-done(((bf16[64,3,2048]{2,1,0:T(4,128)(2,1)}), bf16[64,3,2048]{2,1,0:T(4,128)(2,1)}, u32[]{:S(2)}, u32[]{:S(2)}) %all-to-all-start.16) | async-done | bytes 786464 | tf_op jit(solution)/shard_map/all_to_all | solution.py:45
  580.6 26.7 %all-to-all-done.17 = bf16[64,3,2048]{2,1,0:T(4,128)(2,1)} async-done(((bf16[64,3,2048]{2,1,0:T(4,128)(2,1)}), bf16[64,3,2048]{2,1,0:T(4,128)(2,1)}, u32[]{:S(2)}, u32[]{:S(2)}) %all-to-all-start.17) | async-done | bytes 786464 | tf_op jit(solution)/shard_map/all_to_all | solution.py:52
  642.5 23.4 %all-to-all-done.19 = bf16[64,3,2048]{2,1,0:T(4,128)(2,1)} async-done(((bf16[64,3,2048]{2,1,0:T(4,128)(2,1)}), bf16[64,3,2048]{2,1,0:T(4,128)(2,1)}, u32[]{:S(2)}, u32[]{:S(2)}) %all-to-all-start.19) | async-done | bytes 786464 | tf_op jit(solution)/shard_map/all_to_all | solution.py:45
  701.7 20.6 %all-to-all-done.22 = bf16[64,3,2048]{2,1,0:T(4,128)(2,1)} async-done(((bf16[64,3,2048]{2,1,0:T(4,128)(2,1)}), bf16[64,3,2048]{2,1,0:T(4,128)(2,1)}, u32[]{:S(2)}, u32[]{:S(2)}) %all-to-all-start.22) | async-done | bytes 786464 | tf_op jit(solution)/shard_map/all_to_all | solution.py:60
  750.4 28.5 %all-to-all-done.23 = bf16[64,3,2048]{2,1,0:T(4,128)(2,1)} async-done(((bf16[64,3,2048]{2,1,0:T(4,128)(2,1)}), bf16[64,3,2048]{2,1,0:T(4,128)(2,1)}, u32[]{:S(2)}, u32[]{:S(2)}) %all-to-all-start.23) | async-done | bytes 786464 | tf_op jit(solution)/shard_map/all_to_all | solution.py:56
  788.4 19.0 %all-to-all-done.24 = bf16[64,3,2048]{2,1,0:T(4,128)(2,1)} async-done(((bf16[64,3,2048]{2,1,0:T(4,128)(2,1)}), bf16[64,3,2048]{2,1,0:T(4,128)(2,1)}, u32[]{:S(2)}, u32[]{:S(2)}) %all-to-all-start.24) | async-done | bytes 786464 | tf_op jit(solution)/shard_map/all_to_all | solution.py:60
  839.6 28.5 %all-to-all-done.25 = bf16[64,3,2048]{2,1,0:T(4,128)(2,1)} async-done(((bf16[64,3,2048]{2,1,0:T(4,128)(2,1)}), bf16[64,3,2048]{2,1,0:T(4,128)(2,1)}, u32[]{:S(2)}, u32[]{:S(2)}) %all-to-all-start.25) | async-done | bytes 786464 | tf_op jit(solution)/shard_map/all_to_all | solution.py:56
  877.8 19.0 %all-to-all-done.26 = bf16[64,3,2048]{2,1,0:T(4,128)(2,1)} async-done(((bf16[64,3,2048]{2,1,0:T(4,128)(2,1)}), bf16[64,3,2048]{2,1,0:T(4,128)(2,1)}, u32[]{:S(2)}, u32[]{:S(2)}) %all-to-all-start.26) | async-done | bytes 786464 | tf_op jit(solution)/shard_map/all_to_all | solution.py:60
  930.2 28.5 %all-to-all-done.27 = bf16[64,3,2048]{2,1,0:T(4,128)(2,1)} async-done(((bf16[64,3,2048]{2,1,0:T(4,128)(2,1)}), bf16[64,3,2048]{2,1,0:T(4,128)(2,1)}, u32[]{:S(2)}, u32[]{:S(2)}) %all-to-all-start.27) | async-done | bytes 786464 | tf_op jit(solution)/shard_map/all_to_all | solution.py:56
  976.9 19.1 %all-to-all-done.28 = bf16[64,3,2048]{2,1,0:T(4,128)(2,1)} async-done(((bf16[64,3,2048]{2,1,0:T(4,128)(2,1)}), bf16[64,3,2048]{2,1,0:T(4,128)(2,1)}, u32[]{:S(2)}, u32[]{:S(2)}) %all-to-all-start.28) | async-done | bytes 786464 | tf_op jit(solution)/shard_map/all_to_all | solution.py:60
  1020.2 28.5 %all-to-all-done.29 = bf16[64,3,2048]{2,1,0:T(4,128)(2,1)} async-done(((bf16[64,3,2048]{2,1,0:T(4,128)(2,1)}), bf16[64,3,2048]{2,1,0:T(4,128)(2,1)}, u32[]{:S(2)}, u32[]{:S(2)}) %all-to-all-start.29) | async-done | bytes 786464 | tf_op jit(solution)/shard_map/all_to_all | solution.py:56
  1066.9 19.1 %all-to-all-done.30 = bf16[64,3,2048]{2,1,0:T(4,128)(2,1)} async-done(((bf16[64,3,2048]{2,1,0:T(4,128)(2,1)}), bf16[64,3,2048]{2,1,0:T(4,128)(2,1)}, u32[]{:S(2)}, u32[]{:S(2)}) %all-to-all-start.30) | async-done | bytes 786464 | tf_op jit(solution)/shard_map/all_to_all | solution.py:60
  1091.4 23.4 %collective-permute-done.10 = bf16[32,2048]{1,0:T(8,128)(2,1)S(1)} collective-permute-done((bf16[32,2048]{1,0:T(8,128)(2,1)S(1)}, bf16[32,2048]{1,0:T(8,128)(2,1)S(1)}, u32[]{:S(2)}, u32[]{:S(2)}) %collective-permute-start.10) | collective-permute-done | bytes 131104 | tf_op jit(solution)/shard_map/ppermute | solution.py:13
  1123.6 28.0 %all-to-all-done.31 = bf16[64,3,2048]{2,1,0:T(4,128)(2,1)} async-done(((bf16[64,3,2048]{2,1,0:T(4,128)(2,1)}), bf16[64,3,2048]{2,1,0:T(4,128)(2,1)}, u32[]{:S(2)}, u32[]{:S(2)}) %all-to-all-start.31) | async-done | bytes 786464 | tf_op jit(solution)/shard_map/all_to_all | solution.py:56
  1170.2 27.8 %all-to-all-done.32 = bf16[64,3,2048]{2,1,0:T(4,128)(2,1)} async-done(((bf16[64,3,2048]{2,1,0:T(4,128)(2,1)}), bf16[64,3,2048]{2,1,0:T(4,128)(2,1)}, u32[]{:S(2)}, u32[]{:S(2)}) %all-to-all-start.32) | async-done | bytes 786464 | tf_op jit(solution)/shard_map/all_to_all | solution.py:60
  1302.3 203.1 %psum.7 = f32[1,2048]{1,0:T(1,128)} all-reduce(f32[1,2048]{1,0:T(1,128)S(1)} %bitcast.633), channel_id=1, replica_groups=mesh['dp'=8,'pipe'=4,'expert'=8] {'dp','expert'}, use_global_device_ids=true, to_apply=%region_84.85 | all-reduce | flops 2048 | bytes 16384 | tf_op jit(solution)/shard_map/psum | solution.py:226
  (416 shorter events, 826.0 us)
Async XLA Ops:
  5.5 27.2 %all-to-all-start = ((bf16[64,3,1]{1,2,0:T(2,128)(2,1)}), bf16[64,3,1]{1,2,0:T(2,128)(2,1)S(1)}, u32[]{:S(2)}, u32[]{:S(2)}) async-start(bf16[64,3,1]{1,2,0:T(2,128)(2,1)} %copy.214), calls=%async_computation | async-start | bytes 65536 | tf_op jit(solution)/shard_map/all_to_all | solution.py:46
  32.7 33.2 %all-to-all-start.1 = ((bf16[64,3,2048]{2,1,0:T(4,128)(2,1)}), bf16[64,3,2048]{2,1,0:T(4,128)(2,1)}, u32[]{:S(2)}, u32[]{:S(2)}) async-start(bf16[64,3,2048]{2,1,0:T(4,128)(2,1)} %copy.215), calls=%async_computation.1 | async-start | bytes 2097152 | tf_op jit(solution)/shard_map/all_to_all | solution.py:45
  78.3 24.5 %all-to-all-start.2 = ((bf16[64,3,2048]{2,1,0:T(4,128)(2,1)}), bf16[64,3,2048]{2,1,0:T(4,128)(2,1)}, u32[]{:S(2)}, u32[]{:S(2)}) async-start(bf16[64,3,2048]{2,1,0:T(4,128)(2,1)} %reshape.639), calls=%async_computation.2 | async-start | bytes 2097152 | tf_op jit(solution)/shard_map/all_to_all | solution.py:52
  122.4 43.0 %all-to-all-start.4 = ((bf16[64,3,2048]{2,1,0:T(4,128)(2,1)}), bf16[64,3,2048]{2,1,0:T(4,128)(2,1)}, u32[]{:S(2)}, u32[]{:S(2)}) async-start(bf16[64,3,2048]{2,1,0:T(4,128)(2,1)} %copy.219), calls=%async_computation.4 | async-start | bytes 2097152 | tf_op jit(solution)/shard_map/all_to_all | solution.py:45
  240.8 34.5 %all-to-all-start.7 = ((bf16[64,3,2048]{2,1,0:T(4,128)(2,1)}), bf16[64,3,2048]{2,1,0:T(4,128)(2,1)}, u32[]{:S(2)}, u32[]{:S(2)}) async-start(bf16[64,3,2048]{2,1,0:T(4,128)(2,1)} %copy.223), calls=%async_computation.7 | async-start | bytes 2097152 | tf_op jit(solution)/shard_map/all_to_all | solution.py:45
  287.7 31.1 %all-to-all-start.8 = ((bf16[64,3,2048]{2,1,0:T(4,128)(2,1)}), bf16[64,3,2048]{2,1,0:T(4,128)(2,1)}, u32[]{:S(2)}, u32[]{:S(2)}) async-start(bf16[64,3,2048]{2,1,0:T(4,128)(2,1)} %reshape.643), calls=%async_computation.8 | async-start | bytes 2097152 | tf_op jit(solution)/shard_map/all_to_all | solution.py:52
  345.1 32.7 %all-to-all-start.10 = ((bf16[64,3,2048]{2,1,0:T(4,128)(2,1)}), bf16[64,3,2048]{2,1,0:T(4,128)(2,1)}, u32[]{:S(2)}, u32[]{:S(2)}) async-start(bf16[64,3,2048]{2,1,0:T(4,128)(2,1)} %copy.227), calls=%async_computation.10 | async-start | bytes 2097152 | tf_op jit(solution)/shard_map/all_to_all | solution.py:45
  390.2 31.1 %all-to-all-start.11 = ((bf16[64,3,2048]{2,1,0:T(4,128)(2,1)}), bf16[64,3,2048]{2,1,0:T(4,128)(2,1)}, u32[]{:S(2)}, u32[]{:S(2)}) async-start(bf16[64,3,2048]{2,1,0:T(4,128)(2,1)} %reshape.645), calls=%async_computation.11 | async-start | bytes 2097152 | tf_op jit(solution)/shard_map/all_to_all | solution.py:52
  447.0 27.6 %all-to-all-start.13 = ((bf16[64,3,2048]{2,1,0:T(4,128)(2,1)}), bf16[64,3,2048]{2,1,0:T(4,128)(2,1)}, u32[]{:S(2)}, u32[]{:S(2)}) async-start(bf16[64,3,2048]{2,1,0:T(4,128)(2,1)} %copy.231), calls=%async_computation.13 | async-start | bytes 2097152 | tf_op jit(solution)/shard_map/all_to_all | solution.py:45
  479.9 30.7 %all-to-all-start.14 = ((bf16[64,3,2048]{2,1,0:T(4,128)(2,1)}), bf16[64,3,2048]{2,1,0:T(4,128)(2,1)}, u32[]{:S(2)}, u32[]{:S(2)}) async-start(bf16[64,3,2048]{2,1,0:T(4,128)(2,1)} %reshape.647), calls=%async_computation.14 | async-start | bytes 2097152 | tf_op jit(solution)/shard_map/all_to_all | solution.py:52
  536.3 28.2 %all-to-all-start.16 = ((bf16[64,3,2048]{2,1,0:T(4,128)(2,1)}), bf16[64,3,2048]{2,1,0:T(4,128)(2,1)}, u32[]{:S(2)}, u32[]{:S(2)}) async-start(bf16[64,3,2048]{2,1,0:T(4,128)(2,1)} %copy.235), calls=%async_computation.16 | async-start | bytes 2097152 | tf_op jit(solution)/shard_map/all_to_all | solution.py:45
  569.6 37.7 %all-to-all-start.17 = ((bf16[64,3,2048]{2,1,0:T(4,128)(2,1)}), bf16[64,3,2048]{2,1,0:T(4,128)(2,1)}, u32[]{:S(2)}, u32[]{:S(2)}) async-start(bf16[64,3,2048]{2,1,0:T(4,128)(2,1)} %reshape.649), calls=%async_computation.17 | async-start | bytes 2097152 | tf_op jit(solution)/shard_map/all_to_all | solution.py:52
  631.6 34.4 %all-to-all-start.19 = ((bf16[64,3,2048]{2,1,0:T(4,128)(2,1)}), bf16[64,3,2048]{2,1,0:T(4,128)(2,1)}, u32[]{:S(2)}, u32[]{:S(2)}) async-start(bf16[64,3,2048]{2,1,0:T(4,128)(2,1)} %copy.239), calls=%async_computation.19 | async-start | bytes 2097152 | tf_op jit(solution)/shard_map/all_to_all | solution.py:45
  694.6 27.6 %all-to-all-start.22 = ((bf16[64,3,2048]{2,1,0:T(4,128)(2,1)}), bf16[64,3,2048]{2,1,0:T(4,128)(2,1)}, u32[]{:S(2)}, u32[]{:S(2)}) async-start(bf16[64,3,2048]{2,1,0:T(4,128)(2,1)} %reshape.654), calls=%async_computation.22 | async-start | bytes 2097152 | tf_op jit(solution)/shard_map/all_to_all | solution.py:60
  744.6 34.2 %all-to-all-start.23 = ((bf16[64,3,2048]{2,1,0:T(4,128)(2,1)}), bf16[64,3,2048]{2,1,0:T(4,128)(2,1)}, u32[]{:S(2)}, u32[]{:S(2)}) async-start(bf16[64,3,2048]{2,1,0:T(4,128)(2,1)} %copy.251), calls=%async_computation.23 | async-start | bytes 2097152 | tf_op jit(solution)/shard_map/all_to_all | solution.py:56
  827.4 40.7 %all-to-all-start.25 = ((bf16[64,3,2048]{2,1,0:T(4,128)(2,1)}), bf16[64,3,2048]{2,1,0:T(4,128)(2,1)}, u32[]{:S(2)}, u32[]{:S(2)}) async-start(bf16[64,3,2048]{2,1,0:T(4,128)(2,1)} %copy.253), calls=%async_computation.25 | async-start | bytes 2097152 | tf_op jit(solution)/shard_map/all_to_all | solution.py:56
  922.4 36.3 %all-to-all-start.27 = ((bf16[64,3,2048]{2,1,0:T(4,128)(2,1)}), bf16[64,3,2048]{2,1,0:T(4,128)(2,1)}, u32[]{:S(2)}, u32[]{:S(2)}) async-start(bf16[64,3,2048]{2,1,0:T(4,128)(2,1)} %copy.255), calls=%async_computation.27 | async-start | bytes 2097152 | tf_op jit(solution)/shard_map/all_to_all | solution.py:56
  1012.4 36.3 %all-to-all-start.29 = ((bf16[64,3,2048]{2,1,0:T(4,128)(2,1)}), bf16[64,3,2048]{2,1,0:T(4,128)(2,1)}, u32[]{:S(2)}, u32[]{:S(2)}) async-start(bf16[64,3,2048]{2,1,0:T(4,128)(2,1)} %copy.257), calls=%async_computation.29 | async-start | bytes 2097152 | tf_op jit(solution)/shard_map/all_to_all | solution.py:56
  1090.1 24.7 %collective-permute-start.10 = (bf16[32,2048]{1,0:T(8,128)(2,1)S(1)}, bf16[32,2048]{1,0:T(8,128)(2,1)S(1)}, u32[]{:S(2)}, u32[]{:S(2)}) collective-permute-start(bf16[32,2048]{1,0:T(8,128)(2,1)S(1)} %get-tuple-element.782), channel_id=1, source_target_pairs={{8,0},{16,8},{24,16},{9,1},{17,9},{25,17},{10,2},{18,10},{26,18},{... | collective-permute-start | bytes 393224 | tf_op jit(solution)/shard_map/ppermute | solution.py:13
  1117.9 33.7 %all-to-all-start.31 = ((bf16[64,3,2048]{2,1,0:T(4,128)(2,1)}), bf16[64,3,2048]{2,1,0:T(4,128)(2,1)}, u32[]{:S(2)}, u32[]{:S(2)}) async-start(bf16[64,3,2048]{2,1,0:T(4,128)(2,1)} %copy.259), calls=%async_computation.31 | async-start | bytes 2097152 | tf_op jit(solution)/shard_map/all_to_all | solution.py:56
  1164.6 33.5 %all-to-all-start.32 = ((bf16[64,3,2048]{2,1,0:T(4,128)(2,1)}), bf16[64,3,2048]{2,1,0:T(4,128)(2,1)}, u32[]{:S(2)}, u32[]{:S(2)}) async-start(bf16[64,3,2048]{2,1,0:T(4,128)(2,1)} %reshape.664), calls=%async_computation.32 | async-start | bytes 2097152 | tf_op jit(solution)/shard_map/all_to_all | solution.py:60
  1211.5 31.9 %all-to-all-start.33 = ((bf16[64,3,2048]{2,1,0:T(4,128)(2,1)}), bf16[64,3,2048]{2,1,0:T(4,128)(2,1)}, u32[]{:S(2)}, u32[]{:S(2)}) async-start(bf16[64,3,2048]{2,1,0:T(4,128)(2,1)} %copy.261), calls=%async_computation.33 | async-start | bytes 2097152 | tf_op jit(solution)/shard_map/all_to_all | solution.py:56
  1243.3 29.7 %all-to-all-start.20 = ((bf16[64,3,2048]{2,1,0:T(4,128)(2,1)}), bf16[64,3,2048]{2,1,0:T(4,128)(2,1)}, u32[]{:S(2)}, u32[]{:S(2)}) async-start(bf16[64,3,2048]{2,1,0:T(4,128)(2,1)} %reshape.651), calls=%async_computation.20 | async-start | bytes 2097152 | tf_op jit(solution)/shard_map/all_to_all | solution.py:52
  1273.1 27.2 %all-to-all-start.34 = ((bf16[64,3,2048]{2,1,0:T(4,128)(2,1)}), bf16[64,3,2048]{2,1,0:T(4,128)(2,1)S(1)}, u32[]{:S(2)}, u32[]{:S(2)}) async-start(bf16[64,3,2048]{2,1,0:T(4,128)(2,1)} %reshape.666), calls=%async_computation.34 | async-start | bytes 2097152 | tf_op jit(solution)/shard_map/all_to_all | solution.py:60
  (51 other events, 836.2 us)
where the time goes:
time: 1520 us; the launch traced here: 1510 us
  waiting for transfers between devices  747 us (49%)
  starting transfers between devices  290 us (19%)
  blocking collectives  203 us (13%)
  local copies, waits for them, and re-layouts  141 us (9%)
  matrix products  92.5 us (6%)
  other arithmetic  31.6 us (2%)
    psum x1, blocking collectives, body(): gain_grad = lax.psum(gain_sum, ('dp', 'expert'))  203 us
    all_to_all x7, waiting for transfers between devices, send_rows(): lax.all_to_all(row_block, ('dp', 'expert'), split_axis=0, concat_axis=0,...  177 us
    all_to_all x7, waiting for transfers between devices, send_grads(): lax.all_to_all(row_block, ('dp', 'expert'), split_axis=0, concat_axis=0,...  165 us
    all_to_all x7, waiting for transfers between devices, return_grads(): lax.all_to_all(row_block, ('dp', 'expert'), split_axis=0, concat_axis=0,...  144 us
    all_to_all x7, waiting for transfers between devices, return_rows(): lax.all_to_all(row_block, ('dp', 'expert'), split_axis=0, concat_axis=0,...  138 us
    ppermute x12, waiting for transfers between devices, from_behind(): lax.ppermute(value, axis, [(source, source + steps) for source in range(l...  79.9 us
    all_to_all x7, starting transfers between devices, send_rows(): lax.all_to_all(pair_block, ('dp', 'expert'), split_axis=0, concat_axis=0,...  58 us
    all_to_all x7, starting transfers between devices, send_grads(): lax.all_to_all(row_block, ('dp', 'expert'), split_axis=0, concat_axis=0,...  54.3 us
  transfers between devices with their start and end apart: 47, of which 41 were waited for; matrix products, arithmetic and copies ran while one was open for 5% of the time, Pallas kernels for 0%

commit v1 on v0

--- a/solution.py
+++ b/solution.py
@@ -223,7 +223,7 @@
         gain_sum = gain_sum + gain_term
         if tick_num + 1 < ticks:
             incoming = from_behind(grad_bf, "pipe", -1)
-    gain_grad = lax.psum(gain_sum, ("dp", "expert"))
+    gain_grad = lax.psum(lax.psum(gain_sum, "dp"), "expert")
     segment_out = layer_outs[:MICRO].reshape(1, tok_rows, width)
     segment_grad = grad_outs[:MICRO].reshape(1, tok_rows, width)
     return (segment_out, segment_grad, gain_grad.reshape(1, width))

time: 1520 us -> 1360 us (0.89)
  blocking collectives: 203 us -> 38.5 us
    psum x1 -> x2, blocking collectives: 203 us -> 38.5 us  [body(): gain_grad = lax.psum(lax.psum(gain_sum, 'dp'), 'expert')]
  transfers between devices with their start and end apart: 47 -> 47, of which waited for: 41 -> 41; matrix products, arithmetic and copies ran while one was open for 5% -> 6% of each run, Pallas kernels for 0% -> 0%
where the time goes in v1:
time: 1360 us; the launch traced here: 1340 us
  waiting for transfers between devices  747 us (55%)
  starting transfers between devices  290 us (21%)
  local copies, waits for them, and re-layouts  141 us (10%)
  matrix products  92.5 us (7%)
  blocking collectives  38.5 us (3%)
  other arithmetic  31.6 us (2%)
    all_to_all x7, waiting for transfers between devices, send_rows(): lax.all_to_all(row_block, ('dp', 'expert'), split_axis=0, concat_axis=0,...  177 us
    all_to_all x7, waiting for transfers between devices, send_grads(): lax.all_to_all(row_block, ('dp', 'expert'), split_axis=0, concat_axis=0,...  165 us
    all_to_all x7, waiting for transfers between devices, return_grads(): lax.all_to_all(row_block, ('dp', 'expert'), split_axis=0, concat_axis=0,...  144 us
    all_to_all x7, waiting for transfers between devices, return_rows(): lax.all_to_all(row_block, ('dp', 'expert'), split_axis=0, concat_axis=0,...  138 us
    ppermute x12, waiting for transfers between devices, from_behind(): lax.ppermute(value, axis, [(source, source + steps) for source in range(l...  79.9 us
    all_to_all x7, starting transfers between devices, send_rows(): lax.all_to_all(pair_block, ('dp', 'expert'), split_axis=0, concat_axis=0,...  58 us
    all_to_all x7, starting transfers between devices, send_grads(): lax.all_to_all(row_block, ('dp', 'expert'), split_axis=0, concat_axis=0,...  54.3 us
    all_to_all x7, starting transfers between devices, return_rows(): lax.all_to_all(row_block, ('dp', 'expert'), split_axis=0, concat_axis=0,...  50.9 us
  transfers between devices with their start and end apart: 47, of which 41 were waited for; matrix products, arithmetic and copies ran while one was open for 6% of the time, Pallas kernels for 0%

profile of v1, /device:TPU:1, one launch (start us, length us, event | category | flops | bytes accessed | tf_op | source)
XLA Modules:
  0.0 1343.2 jit_solution(13355156007193338560)
XLA Ops:
  40.4 25.5 %all-to-all-done.1 = bf16[64,3,2048]{2,1,0:T(4,128)(2,1)} async-done(((bf16[64,3,2048]{2,1,0:T(4,128)(2,1)}), bf16[64,3,2048]{2,1,0:T(4,128)(2,1)}, u32[]{:S(2)}, u32[]{:S(2)}) %all-to-all-start.1) | async-done | bytes 786464 | tf_op jit(solution)/shard_map/all_to_all | solution.py:45
  136.9 28.5 %all-to-all-done.4 = bf16[64,3,2048]{2,1,0:T(4,128)(2,1)} async-done(((bf16[64,3,2048]{2,1,0:T(4,128)(2,1)}), bf16[64,3,2048]{2,1,0:T(4,128)(2,1)}, u32[]{:S(2)}, u32[]{:S(2)}) %all-to-all-start.4) | async-done | bytes 786464 | tf_op jit(solution)/shard_map/all_to_all | solution.py:45
  246.7 28.6 %all-to-all-done.7 = bf16[64,3,2048]{2,1,0:T(4,128)(2,1)} async-done(((bf16[64,3,2048]{2,1,0:T(4,128)(2,1)}), bf16[64,3,2048]{2,1,0:T(4,128)(2,1)}, u32[]{:S(2)}, u32[]{:S(2)}) %all-to-all-start.7) | async-done | bytes 786464 | tf_op jit(solution)/shard_map/all_to_all | solution.py:45
  298.6 20.2 %all-to-all-done.8 = bf16[64,3,2048]{2,1,0:T(4,128)(2,1)} async-done(((bf16[64,3,2048]{2,1,0:T(4,128)(2,1)}), bf16[64,3,2048]{2,1,0:T(4,128)(2,1)}, u32[]{:S(2)}, u32[]{:S(2)}) %all-to-all-start.8) | async-done | bytes 786464 | tf_op jit(solution)/shard_map/all_to_all | solution.py:52
  350.9 26.9 %all-to-all-done.10 = bf16[64,3,2048]{2,1,0:T(4,128)(2,1)} async-done(((bf16[64,3,2048]{2,1,0:T(4,128)(2,1)}), bf16[64,3,2048]{2,1,0:T(4,128)(2,1)}, u32[]{:S(2)}, u32[]{:S(2)}) %all-to-all-start.10) | async-done | bytes 786464 | tf_op jit(solution)/shard_map/all_to_all | solution.py:45
  399.7 21.5 %all-to-all-done.11 = bf16[64,3,2048]{2,1,0:T(4,128)(2,1)} async-done(((bf16[64,3,2048]{2,1,0:T(4,128)(2,1)}), bf16[64,3,2048]{2,1,0:T(4,128)(2,1)}, u32[]{:S(2)}, u32[]{:S(2)}) %all-to-all-start.11) | async-done | bytes 786464 | tf_op jit(solution)/shard_map/all_to_all | solution.py:52
  452.8 21.8 %all-to-all-done.13 = bf16[64,3,2048]{2,1,0:T(4,128)(2,1)} async-done(((bf16[64,3,2048]{2,1,0:T(4,128)(2,1)}), bf16[64,3,2048]{2,1,0:T(4,128)(2,1)}, u32[]{:S(2)}, u32[]{:S(2)}) %all-to-all-start.13) | async-done | bytes 786464 | tf_op jit(solution)/shard_map/all_to_all | solution.py:45
  486.5 24.1 %all-to-all-done.14 = bf16[64,3,2048]{2,1,0:T(4,128)(2,1)} async-done(((bf16[64,3,2048]{2,1,0:T(4,128)(2,1)}), bf16[64,3,2048]{2,1,0:T(4,128)(2,1)}, u32[]{:S(2)}, u32[]{:S(2)}) %all-to-all-start.14) | async-done | bytes 786464 | tf_op jit(solution)/shard_map/all_to_all | solution.py:52
  542.1 22.4 %all-to-all-done.16 = bf16[64,3,2048]{2,1,0:T(4,128)(2,1)} async-done(((bf16[64,3,2048]{2,1,0:T(4,128)(2,1)}), bf16[64,3,2048]{2,1,0:T(4,128)(2,1)}, u32[]{:S(2)}, u32[]{:S(2)}) %all-to-all-start.16) | async-done | bytes 786464 | tf_op jit(solution)/shard_map/all_to_all | solution.py:45
  580.6 26.7 %all-to-all-done.17 = bf16[64,3,2048]{2,1,0:T(4,128)(2,1)} async-done(((bf16[64,3,2048]{2,1,0:T(4,128)(2,1)}), bf16[64,3,2048]{2,1,0:T(4,128)(2,1)}, u32[]{:S(2)}, u32[]{:S(2)}) %all-to-all-start.17) | async-done | bytes 786464 | tf_op jit(solution)/shard_map/all_to_all | solution.py:52
  642.5 23.4 %all-to-all-done.19 = bf16[64,3,2048]{2,1,0:T(4,128)(2,1)} async-done(((bf16[64,3,2048]{2,1,0:T(4,128)(2,1)}), bf16[64,3,2048]{2,1,0:T(4,128)(2,1)}, u32[]{:S(2)}, u32[]{:S(2)}) %all-to-all-start.19) | async-done | bytes 786464 | tf_op jit(solution)/shard_map/all_to_all | solution.py:45
  701.7 20.6 %all-to-all-done.22 = bf16[64,3,2048]{2,1,0:T(4,128)(2,1)} async-done(((bf16[64,3,2048]{2,1,0:T(4,128)(2,1)}), bf16[64,3,2048]{2,1,0:T(4,128)(2,1)}, u32[]{:S(2)}, u32[]{:S(2)}) %all-to-all-start.22) | async-done | bytes 786464 | tf_op jit(solution)/shard_map/all_to_all | solution.py:60
  750.4 28.5 %all-to-all-done.23 = bf16[64,3,2048]{2,1,0:T(4,128)(2,1)} async-done(((bf16[64,3,2048]{2,1,0:T(4,128)(2,1)}), bf16[64,3,2048]{2,1,0:T(4,128)(2,1)}, u32[]{:S(2)}, u32[]{:S(2)}) %all-to-all-start.23) | async-done | bytes 786464 | tf_op jit(solution)/shard_map/all_to_all | solution.py:56
  788.4 19.0 %all-to-all-done.24 = bf16[64,3,2048]{2,1,0:T(4,128)(2,1)} async-done(((bf16[64,3,2048]{2,1,0:T(4,128)(2,1)}), bf16[64,3,2048]{2,1,0:T(4,128)(2,1)}, u32[]{:S(2)}, u32[]{:S(2)}) %all-to-all-start.24) | async-done | bytes 786464 | tf_op jit(solution)/shard_map/all_to_all | solution.py:60
  839.6 28.5 %all-to-all-done.25 = bf16[64,3,2048]{2,1,0:T(4,128)(2,1)} async-done(((bf16[64,3,2048]{2,1,0:T(4,128)(2,1)}), bf16[64,3,2048]{2,1,0:T(4,128)(2,1)}, u32[]{:S(2)}, u32[]{:S(2)}) %all-to-all-start.25) | async-done | bytes 786464 | tf_op jit(solution)/shard_map/all_to_all | solution.py:56
  877.8 19.0 %all-to-all-done.26 = bf16[64,3,2048]{2,1,0:T(4,128)(2,1)} async-done(((bf16[64,3,2048]{2,1,0:T(4,128)(2,1)}), bf16[64,3,2048]{2,1,0:T(4,128)(2,1)}, u32[]{:S(2)}, u32[]{:S(2)}) %all-to-all-start.26) | async-done | bytes 786464 | tf_op jit(solution)/shard_map/all_to_all | solution.py:60
  930.2 28.5 %all-to-all-done.27 = bf16[64,3,2048]{2,1,0:T(4,128)(2,1)} async-done(((bf16[64,3,2048]{2,1,0:T(4,128)(2,1)}), bf16[64,3,2048]{2,1,0:T(4,128)(2,1)}, u32[]{:S(2)}, u32[]{:S(2)}) %all-to-all-start.27) | async-done | bytes 786464 | tf_op jit(solution)/shard_map/all_to_all | solution.py:56
  976.9 19.1 %all-to-all-done.28 = bf16[64,3,2048]{2,1,0:T(4,128)(2,1)} async-done(((bf16[64,3,2048]{2,1,0:T(4,128)(2,1)}), bf16[64,3,2048]{2,1,0:T(4,128)(2,1)}, u32[]{:S(2)}, u32[]{:S(2)}) %all-to-all-start.28) | async-done | bytes 786464 | tf_op jit(solution)/shard_map/all_to_all | solution.py:60
  1020.2 28.5 %all-to-all-done.29 = bf16[64,3,2048]{2,1,0:T(4,128)(2,1)} async-done(((bf16[64,3,2048]{2,1,0:T(4,128)(2,1)}), bf16[64,3,2048]{2,1,0:T(4,128)(2,1)}, u32[]{:S(2)}, u32[]{:S(2)}) %all-to-all-start.29) | async-done | bytes 786464 | tf_op jit(solution)/shard_map/all_to_all | solution.py:56
  1066.9 19.1 %all-to-all-done.30 = bf16[64,3,2048]{2,1,0:T(4,128)(2,1)} async-done(((bf16[64,3,2048]{2,1,0:T(4,128)(2,1)}), bf16[64,3,2048]{2,1,0:T(4,128)(2,1)}, u32[]{:S(2)}, u32[]{:S(2)}) %all-to-all-start.30) | async-done | bytes 786464 | tf_op jit(solution)/shard_map/all_to_all | solution.py:60
  1091.4 23.4 %collective-permute-done.10 = bf16[32,2048]{1,0:T(8,128)(2,1)S(1)} collective-permute-done((bf16[32,2048]{1,0:T(8,128)(2,1)S(1)}, bf16[32,2048]{1,0:T(8,128)(2,1)S(1)}, u32[]{:S(2)}, u32[]{:S(2)}) %collective-permute-start.10) | collective-permute-done | bytes 131104 | tf_op jit(solution)/shard_map/ppermute | solution.py:13
  1123.6 28.0 %all-to-all-done.31 = bf16[64,3,2048]{2,1,0:T(4,128)(2,1)} async-done(((bf16[64,3,2048]{2,1,0:T(4,128)(2,1)}), bf16[64,3,2048]{2,1,0:T(4,128)(2,1)}, u32[]{:S(2)}, u32[]{:S(2)}) %all-to-all-start.31) | async-done | bytes 786464 | tf_op jit(solution)/shard_map/all_to_all | solution.py:56
  1170.2 27.8 %all-to-all-done.32 = bf16[64,3,2048]{2,1,0:T(4,128)(2,1)} async-done(((bf16[64,3,2048]{2,1,0:T(4,128)(2,1)}), bf16[64,3,2048]{2,1,0:T(4,128)(2,1)}, u32[]{:S(2)}, u32[]{:S(2)}) %all-to-all-start.32) | async-done | bytes 786464 | tf_op jit(solution)/shard_map/all_to_all | solution.py:60
  1302.3 21.5 %psum.14 = f32[2048]{0:T(1024)S(1)} all-reduce(f32[2048]{0:T(1024)S(1)} %select_add_fusion), channel_id=1, replica_groups=mesh['dp'=8,'pipe'=4,'expert'=8] {'dp'}, use_global_device_ids=true, to_apply=%region_84.85 | all-reduce | flops 2048 | bytes 16384 | tf_op jit(solution)/shard_map/psum | solution.py:226
  (417 shorter events, 843.0 us)
Async XLA Ops:
  5.5 27.2 %all-to-all-start = ((bf16[64,3,1]{1,2,0:T(2,128)(2,1)}), bf16[64,3,1]{1,2,0:T(2,128)(2,1)S(1)}, u32[]{:S(2)}, u32[]{:S(2)}) async-start(bf16[64,3,1]{1,2,0:T(2,128)(2,1)} %copy.214), calls=%async_computation | async-start | bytes 65536 | tf_op jit(solution)/shard_map/all_to_all | solution.py:46
  32.7 33.2 %all-to-all-start.1 = ((bf16[64,3,2048]{2,1,0:T(4,128)(2,1)}), bf16[64,3,2048]{2,1,0:T(4,128)(2,1)}, u32[]{:S(2)}, u32[]{:S(2)}) async-start(bf16[64,3,2048]{2,1,0:T(4,128)(2,1)} %copy.215), calls=%async_computation.1 | async-start | bytes 2097152 | tf_op jit(solution)/shard_map/all_to_all | solution.py:45
  78.3 24.5 %all-to-all-start.2 = ((bf16[64,3,2048]{2,1,0:T(4,128)(2,1)}), bf16[64,3,2048]{2,1,0:T(4,128)(2,1)}, u32[]{:S(2)}, u32[]{:S(2)}) async-start(bf16[64,3,2048]{2,1,0:T(4,128)(2,1)} %reshape.639), calls=%async_computation.2 | async-start | bytes 2097152 | tf_op jit(solution)/shard_map/all_to_all | solution.py:52
  122.4 43.0 %all-to-all-start.4 = ((bf16[64,3,2048]{2,1,0:T(4,128)(2,1)}), bf16[64,3,2048]{2,1,0:T(4,128)(2,1)}, u32[]{:S(2)}, u32[]{:S(2)}) async-start(bf16[64,3,2048]{2,1,0:T(4,128)(2,1)} %copy.219), calls=%async_computation.4 | async-start | bytes 2097152 | tf_op jit(solution)/shard_map/all_to_all | solution.py:45
  240.8 34.5 %all-to-all-start.7 = ((bf16[64,3,2048]{2,1,0:T(4,128)(2,1)}), bf16[64,3,2048]{2,1,0:T(4,128)(2,1)}, u32[]{:S(2)}, u32[]{:S(2)}) async-start(bf16[64,3,2048]{2,1,0:T(4,128)(2,1)} %copy.223), calls=%async_computation.7 | async-start | bytes 2097152 | tf_op jit(solution)/shard_map/all_to_all | solution.py:45
  287.7 31.1 %all-to-all-start.8 = ((bf16[64,3,2048]{2,1,0:T(4,128)(2,1)}), bf16[64,3,2048]{2,1,0:T(4,128)(2,1)}, u32[]{:S(2)}, u32[]{:S(2)}) async-start(bf16[64,3,2048]{2,1,0:T(4,128)(2,1)} %reshape.643), calls=%async_computation.8 | async-start | bytes 2097152 | tf_op jit(solution)/shard_map/all_to_all | solution.py:52
  345.1 32.7 %all-to-all-start.10 = ((bf16[64,3,2048]{2,1,0:T(4,128)(2,1)}), bf16[64,3,2048]{2,1,0:T(4,128)(2,1)}, u32[]{:S(2)}, u32[]{:S(2)}) async-start(bf16[64,3,2048]{2,1,0:T(4,128)(2,1)} %copy.227), calls=%async_computation.10 | async-start | bytes 2097152 | tf_op jit(solution)/shard_map/all_to_all | solution.py:45
  390.2 31.1 %all-to-all-start.11 = ((bf16[64,3,2048]{2,1,0:T(4,128)(2,1)}), bf16[64,3,2048]{2,1,0:T(4,128)(2,1)}, u32[]{:S(2)}, u32[]{:S(2)}) async-start(bf16[64,3,2048]{2,1,0:T(4,128)(2,1)} %reshape.645), calls=%async_computation.11 | async-start | bytes 2097152 | tf_op jit(solution)/shard_map/all_to_all | solution.py:52
  447.0 27.6 %all-to-all-start.13 = ((bf16[64,3,2048]{2,1,0:T(4,128)(2,1)}), bf16[64,3,2048]{2,1,0:T(4,128)(2,1)}, u32[]{:S(2)}, u32[]{:S(2)}) async-start(bf16[64,3,2048]{2,1,0:T(4,128)(2,1)} %copy.231), calls=%async_computation.13 | async-start | bytes 2097152 | tf_op jit(solution)/shard_map/all_to_all | solution.py:45
  479.9 30.7 %all-to-all-start.14 = ((bf16[64,3,2048]{2,1,0:T(4,128)(2,1)}), bf16[64,3,2048]{2,1,0:T(4,128)(2,1)}, u32[]{:S(2)}, u32[]{:S(2)}) async-start(bf16[64,3,2048]{2,1,0:T(4,128)(2,1)} %reshape.647), calls=%async_computation.14 | async-start | bytes 2097152 | tf_op jit(solution)/shard_map/all_to_all | solution.py:52
  536.3 28.2 %all-to-all-start.16 = ((bf16[64,3,2048]{2,1,0:T(4,128)(2,1)}), bf16[64,3,2048]{2,1,0:T(4,128)(2,1)}, u32[]{:S(2)}, u32[]{:S(2)}) async-start(bf16[64,3,2048]{2,1,0:T(4,128)(2,1)} %copy.235), calls=%async_computation.16 | async-start | bytes 2097152 | tf_op jit(solution)/shard_map/all_to_all | solution.py:45
  569.6 37.7 %all-to-all-start.17 = ((bf16[64,3,2048]{2,1,0:T(4,128)(2,1)}), bf16[64,3,2048]{2,1,0:T(4,128)(2,1)}, u32[]{:S(2)}, u32[]{:S(2)}) async-start(bf16[64,3,2048]{2,1,0:T(4,128)(2,1)} %reshape.649), calls=%async_computation.17 | async-start | bytes 2097152 | tf_op jit(solution)/shard_map/all_to_all | solution.py:52
  631.6 34.4 %all-to-all-start.19 = ((bf16[64,3,2048]{2,1,0:T(4,128)(2,1)}), bf16[64,3,2048]{2,1,0:T(4,128)(2,1)}, u32[]{:S(2)}, u32[]{:S(2)}) async-start(bf16[64,3,2048]{2,1,0:T(4,128)(2,1)} %copy.239), calls=%async_computation.19 | async-start | bytes 2097152 | tf_op jit(solution)/shard_map/all_to_all | solution.py:45
  694.6 27.6 %all-to-all-start.22 = ((bf16[64,3,2048]{2,1,0:T(4,128)(2,1)}), bf16[64,3,2048]{2,1,0:T(4,128)(2,1)}, u32[]{:S(2)}, u32[]{:S(2)}) async-start(bf16[64,3,2048]{2,1,0:T(4,128)(2,1)} %reshape.654), calls=%async_computation.22 | async-start | bytes 2097152 | tf_op jit(solution)/shard_map/all_to_all | solution.py:60
  744.6 34.2 %all-to-all-start.23 = ((bf16[64,3,2048]{2,1,0:T(4,128)(2,1)}), bf16[64,3,2048]{2,1,0:T(4,128)(2,1)}, u32[]{:S(2)}, u32[]{:S(2)}) async-start(bf16[64,3,2048]{2,1,0:T(4,128)(2,1)} %copy.251), calls=%async_computation.23 | async-start | bytes 2097152 | tf_op jit(solution)/shard_map/all_to_all | solution.py:56
  827.4 40.7 %all-to-all-start.25 = ((bf16[64,3,2048]{2,1,0:T(4,128)(2,1)}), bf16[64,3,2048]{2,1,0:T(4,128)(2,1)}, u32[]{:S(2)}, u32[]{:S(2)}) async-start(bf16[64,3,2048]{2,1,0:T(4,128)(2,1)} %copy.253), calls=%async_computation.25 | async-start | bytes 2097152 | tf_op jit(solution)/shard_map/all_to_all | solution.py:56
  922.4 36.3 %all-to-all-start.27 = ((bf16[64,3,2048]{2,1,0:T(4,128)(2,1)}), bf16[64,3,2048]{2,1,0:T(4,128)(2,1)}, u32[]{:S(2)}, u32[]{:S(2)}) async-start(bf16[64,3,2048]{2,1,0:T(4,128)(2,1)} %copy.255), calls=%async_computation.27 | async-start | bytes 2097152 | tf_op jit(solution)/shard_map/all_to_all | solution.py:56
  1012.4 36.3 %all-to-all-start.29 = ((bf16[64,3,2048]{2,1,0:T(4,128)(2,1)}), bf16[64,3,2048]{2,1,0:T(4,128)(2,1)}, u32[]{:S(2)}, u32[]{:S(2)}) async-start(bf16[64,3,2048]{2,1,0:T(4,128)(2,1)} %copy.257), calls=%async_computation.29 | async-start | bytes 2097152 | tf_op jit(solution)/shard_map/all_to_all | solution.py:56
  1090.1 24.7 %collective-permute-start.10 = (bf16[32,2048]{1,0:T(8,128)(2,1)S(1)}, bf16[32,2048]{1,0:T(8,128)(2,1)S(1)}, u32[]{:S(2)}, u32[]{:S(2)}) collective-permute-start(bf16[32,2048]{1,0:T(8,128)(2,1)S(1)} %get-tuple-element.782), channel_id=1, source_target_pairs={{8,0},{16,8},{24,16},{9,1},{17,9},{25,17},{10,2},{18,10},{26,18},{... | collective-permute-start | bytes 393224 | tf_op jit(solution)/shard_map/ppermute | solution.py:13
  1117.9 33.7 %all-to-all-start.31 = ((bf16[64,3,2048]{2,1,0:T(4,128)(2,1)}), bf16[64,3,2048]{2,1,0:T(4,128)(2,1)}, u32[]{:S(2)}, u32[]{:S(2)}) async-start(bf16[64,3,2048]{2,1,0:T(4,128)(2,1)} %copy.259), calls=%async_computation.31 | async-start | bytes 2097152 | tf_op jit(solution)/shard_map/all_to_all | solution.py:56
  1164.6 33.5 %all-to-all-start.32 = ((bf16[64,3,2048]{2,1,0:T(4,128)(2,1)}), bf16[64,3,2048]{2,1,0:T(4,128)(2,1)}, u32[]{:S(2)}, u32[]{:S(2)}) async-start(bf16[64,3,2048]{2,1,0:T(4,128)(2,1)} %reshape.664), calls=%async_computation.32 | async-start | bytes 2097152 | tf_op jit(solution)/shard_map/all_to_all | solution.py:60
  1211.5 31.9 %all-to-all-start.33 = ((bf16[64,3,2048]{2,1,0:T(4,128)(2,1)}), bf16[64,3,2048]{2,1,0:T(4,128)(2,1)}, u32[]{:S(2)}, u32[]{:S(2)}) async-start(bf16[64,3,2048]{2,1,0:T(4,128)(2,1)} %copy.261), calls=%async_computation.33 | async-start | bytes 2097152 | tf_op jit(solution)/shard_map/all_to_all | solution.py:56
  1243.3 29.7 %all-to-all-start.20 = ((bf16[64,3,2048]{2,1,0:T(4,128)(2,1)}), bf16[64,3,2048]{2,1,0:T(4,128)(2,1)}, u32[]{:S(2)}, u32[]{:S(2)}) async-start(bf16[64,3,2048]{2,1,0:T(4,128)(2,1)} %reshape.651), calls=%async_computation.20 | async-start | bytes 2097152 | tf_op jit(solution)/shard_map/all_to_all | solution.py:52
  1273.1 27.2 %all-to-all-start.34 = ((bf16[64,3,2048]{2,1,0:T(4,128)(2,1)}), bf16[64,3,2048]{2,1,0:T(4,128)(2,1)S(1)}, u32[]{:S(2)}, u32[]{:S(2)}) async-start(bf16[64,3,2048]{2,1,0:T(4,128)(2,1)} %reshape.666), calls=%async_computation.34 | async-start | bytes 2097152 | tf_op jit(solution)/shard_map/all_to_all | solution.py:60
  (51 other events, 671.6 us)
